TPU v7x, 512 devices: a whole 4x8x8 slice. The times are simulated.
512 devices in a mesh: section: 2 (over core), tensor: 32 (over z, x), dp: 8 (over y).
Axes of the slice: x: 4, y: 8, z: 8, core: 2. Of those that a mesh axis runs over, the one named last changes fastest.
Arguments:
- grad_out: bfloat16 [2048, 6144], P('dp', 'tensor'), may hold values from -6 to 6
- queries: bfloat16 [2, 2048, 4096], P('section', 'dp', 'tensor'), may hold values from -40 to 40
- key_rows: bfloat16 [2, 2048, 4096], P('section', 'dp', 'tensor'), may hold values from -40 to 40
- value_rows: bfloat16 [2, 2048, 4096], P('section', 'dp', 'tensor'), may hold values from -6 to 6
- w_qkv: bfloat16 [2, 6144, 12288], P('section', 'dp', 'tensor'), may hold values from -0.078125 to 0.078125
- w_out: bfloat16 [2, 4096, 6144], P('section', 'tensor', 'dp'), may hold values from -0.09375 to 0.09375
- seg_lengths: int32 [8, 3], P('dp'), may hold values from 0 to 128, as said below
Outputs:
- input_grad: bfloat16 [2, 2048, 6144], P('section', 'dp', 'tensor')
- out_weight_grad: bfloat16 [2, 4096, 6144], P('section', 'tensor', 'dp')
Inputs may be any that keep to these rules, and one draw needn't show every extreme that they name: `seg_lengths`: each row sums to 256, holds one image of exactly 128 patches and either a second of 128 patches and an empty last slot, or two of 64 patches.
All inputs are finite; a program needn't handle non-finite values.
Results may differ from a plain program's by a relative error of at most 0.023.
Values may be sent and summed in bfloat16 or wider, within the bound.
A program may use at most 64 MiB of HBM per device.

v0:
```python
import jax
import jax.numpy as jnp
from jax import lax
from jax.sharding import PartitionSpec as P

PACK = 256
MB = 1
negative_big = -1e30


def passed_along(value, axis, steps):
    count = lax.axis_size(axis)
    first, last = (max(0, -steps), min(count, count - steps))
    return lax.ppermute(value, axis, [(source, source + steps) for source in range(first, last)])


def contract(left, right, left_dim, right_dim):
    return lax.dot_general(
        left, right, (((left_dim,), (right_dim,)), ((), ())), preferred_element_type=jnp.float32
    )


def attend_back(query_blk, key_blk, value_blk, grad_attn, same_seg, scaling):
    scores = contract(query_blk, key_blk, 1, 1) * scaling
    scores = jnp.where(same_seg, scores, negative_big)
    peak = jnp.max(scores, axis=-1, keepdims=True)
    shifted = jnp.exp(scores - peak)
    probs = shifted / jnp.sum(shifted, axis=-1, keepdims=True)
    probs_low = probs.astype(jnp.bfloat16)
    attended = jnp.dot(probs_low, value_blk, preferred_element_type=jnp.float32).astype(
        jnp.bfloat16
    )
    grad_value = contract(probs_low, grad_attn, 0, 0).astype(jnp.bfloat16)
    grad_probs = contract(grad_attn, value_blk, 1, 1)
    centred = jnp.sum(probs * grad_probs, axis=-1, keepdims=True)
    grad_scores = (probs * (grad_probs - centred) * scaling).astype(jnp.bfloat16)
    grad_query = jnp.dot(grad_scores, key_blk, preferred_element_type=jnp.float32).astype(
        jnp.bfloat16
    )
    grad_key = contract(grad_scores, query_blk, 0, 0).astype(jnp.bfloat16)
    return (attended, grad_query, grad_key, grad_value)


def per_device(grad_out, queries, key_rows, value_rows, w_qkv, w_out, seg_lengths):
    sections = lax.axis_size("section")
    section_index = lax.axis_index("section")
    head_index = lax.axis_index("tensor")
    width = grad_out.shape[1]
    qkv_full, out_full = (
        lax.all_gather(w_qkv, "dp", axis=1, tiled=True),
        lax.all_gather(w_out, "dp", axis=2, tiled=True),
    )
    proj_in = qkv_full[0]
    proj_out = out_full[0]
    head_dim = proj_out.shape[0]
    full_width = proj_out.shape[1]
    scaling = head_dim ** (-0.5)
    seg_ends = jnp.cumsum(seg_lengths, axis=1)
    position = jnp.arange(PACK, dtype=jnp.int32)
    seg_table = jnp.sum((position[None, :, None] >= seg_ends[:, None, :]).astype(jnp.int32), axis=2)
    offset = sections - 1 - section_index
    carried = jnp.zeros((PACK, width), jnp.bfloat16)
    result = jnp.zeros((MB * PACK, width), jnp.bfloat16)
    grad_acc = jnp.zeros((head_dim, full_width), jnp.float32)
    for step_index in range(MB + sections - 1):
        micro = step_index - offset
        active = (micro >= 0) & (micro < MB)
        which = jnp.clip(micro, 0, MB - 1)
        incoming = jnp.where(section_index == sections - 1, grad_out, carried)
        whole = lax.all_gather(incoming, "tensor", axis=1, tiled=True)
        query_blk = queries[0]
        key_blk = key_rows[0]
        value_blk = value_rows[0]
        seg_ids = lax.dynamic_index_in_dim(seg_table, which, 0, keepdims=False)
        same_seg = seg_ids[:, None] == seg_ids[None, :]
        grad_attn = contract(whole, proj_out, 1, 1).astype(jnp.bfloat16)
        attended, grad_query, grad_key, grad_value = attend_back(
            query_blk, key_blk, value_blk, grad_attn, same_seg, scaling
        )
        combined = jnp.concatenate([grad_query, grad_key, grad_value], axis=1)
        head_term = contract(combined, proj_in, 1, 1)
        summed = lax.psum(head_term.astype(jnp.bfloat16), "tensor").astype(jnp.float32)
        share = lax.dynamic_slice_in_dim(summed, head_index * width, width, 1)
        block_grad = (incoming.astype(jnp.float32) + share).astype(jnp.bfloat16)
        result = jnp.where(active, block_grad, result)
        grad_acc = grad_acc + jnp.where(active, contract(attended, whole, 0, 0), 0.0)
        carried = passed_along(block_grad, "section", -1)
    weight_share = lax.psum_scatter(
        grad_acc.astype(jnp.bfloat16), "dp", scatter_dimension=1, tiled=True
    )
    return (result[None], weight_share[None])


def solution(mesh):
    return jax.shard_map(
        per_device,
        mesh=mesh,
        in_specs=(
            P("dp", "tensor"),
            P("section", "dp", "tensor"),
            P("section", "dp", "tensor"),
            P("section", "dp", "tensor"),
            P("section", "dp", "tensor"),
            P("section", "tensor", "dp"),
            P("dp", None),
        ),
        out_specs=(P("section", "dp", "tensor"), P("section", "tensor", "dp")),
        check_vma=False,
    )
```

profile of v0, /device:TPU:6, one launch (start us, length us, event | category | flops | bytes accessed | tf_op | source)
XLA Modules:
  0.0 695.8 jit_solution(12003352529557310799)
XLA Ops:
  7.2 0.0 copy-start
  7.2 0.0 all-gather.7.cloned.1.call-start
  7.2 0.7 all-gather.7.cloned.1.call-update
  7.9 0.0 all-gather.5.cloned.1.call-start
  8.0 0.7 broadcast_select_fusion.1
  8.6 0.0 all-gather.5.cloned.1.call-update
  8.7 0.0 all-gather.9.cloned.1.call-start
  8.7 0.7 all-gather.9.cloned.1.call-update
  9.4 0.0 all-reduce.3.cloned.1.call-start
  9.4 0.8 reduce_window_sum.11
  10.3 0.1 fusion.40
  10.4 1.1 fusion.49
  11.5 0.1 fusion.16
  11.5 0.0 copy-start.8
  11.5 0.0 copy-start.9
  11.5 45.2 %all-gather.7.cloned.1.call-done = bf16[1,128,6144]{2,1,0:T(8,128)(2,1)} async-done(((bf16[1,128,768]{2,1,0:T(8,128)(2,1)}), bf16[1,128,6144]{2,1,0:T(8,128)(2,1)}) %all-gather.7.cloned.1.call-update) | async-done | bytes 1572880 | tf_op jit(solution)/shard_map/all_gather | solution.py:51
  56.7 86.7 %all-gather.5.cloned.1.call-done = bf16[256,6144]{0,1:T(8,128)(2,1)} async-done(((bf16[256,192]{0,1:T(8,128)(2,1)}), bf16[256,6144]{0,1:T(8,128)(2,1)}) %all-gather.5.cloned.1.call-update) | async-done | bytes 3145744 | tf_op jit(solution)/shard_map/all_gather | solution.py:70
  143.4 3.4 fusion.9
  146.8 0.0 copy-done
  146.8 0.2 multiply_reduce_fusion.1
  147.1 0.1 multiply_convert_fusion.1
  147.1 0.0 copy-done.8
  147.1 0.2 convolution_convert_fusion.7
  147.3 0.0 copy-done.9
  147.3 0.2 convolution_convert_fusion.8
  147.6 0.2 convolution_convert_fusion.6
  147.7 57.7 %all-gather.9.cloned.1.call-done = bf16[1,6144,384]{2,1,0:T(8,128)(2,1)} async-done(((bf16[1,768,384]{2,1,0:T(8,128)(2,1)}), bf16[1,6144,384]{2,1,0:T(8,128)(2,1)}) %all-gather.9.cloned.1.call-update) | async-done | bytes 4718608 | tf_op jit(solution)/shard_map/all_gather | solution.py:50
  205.5 5.9 convolution_convert_fusion.1
  211.4 0.0 copy-start.4
  211.4 0.0 copy-start.3
  211.4 0.0 all-reduce.3.cloned.1.call-update
  211.4 0.0 all-gather.11.cloned.1.call-start
  211.5 168.1 %all-reduce.3.cloned.1.call-done = bf16[256,6144]{0,1:T(8,128)(2,1)} async-done(((bf16[256,6144]{0,1:T(8,128)(2,1)}), bf16[256,6144]{0,1:T(8,128)(2,1)}) %all-reduce.3.cloned.1.call-update) | async-done | bytes 3145744 | tf_op jit(solution)/shard_map/psum | solution.py:82
  379.6 0.0 copy-done.4
  379.6 0.9 add_convert_fusion.1
  380.5 0.0 copy-start.6
  380.5 1.3 collective-permute-start
  381.8 1.9 collective-permute-done
  383.7 0.7 broadcast_select_fusion
  384.4 0.0 all-gather.11.cloned.1.call-update
  384.4 0.0 all-reduce.5.cloned.1.call-start
  384.4 82.7 %all-gather.11.cloned.1.call-done = bf16[256,6144]{0,1:T(8,128)(2,1)} async-done(((bf16[256,192]{0,1:T(8,128)(2,1)}), bf16[256,6144]{0,1:T(8,128)(2,1)}) %all-gather.11.cloned.1.call-update) | async-done | bytes 3145744 | tf_op jit(solution)/shard_map/all_gather | solution.py:70
  467.2 0.0 copy-done.3
  467.2 2.9 fusion.12
  470.1 0.2 convolution_convert_fusion.3
  470.3 0.2 multiply_reduce_fusion
  470.5 0.0 copy-done.6
  470.5 0.1 multiply_convert_fusion
  470.6 0.2 convolution_convert_fusion.4
  470.8 0.2 convolution_convert_fusion.5
  471.0 5.9 convolution_convert_fusion
  477.0 0.0 all-reduce.5.cloned.1.call-update
  477.0 0.0 reduce-scatter.2.cloned.1.call-start
  477.0 0.2 convolution_convert_fusion.2
  477.3 1.6 copy-done.1
  478.8 1.2 convolution_select_fusion.1
  480.0 0.7 copy-done.2
  480.7 2.3 fusion.1
  483.1 0.0 reduce-scatter.2.cloned.1.call-update
  483.1 160.8 %all-reduce.5.cloned.1.call-done = bf16[256,6144]{0,1:T(8,128)(2,1)} async-done(((bf16[256,6144]{0,1:T(8,128)(2,1)}), bf16[256,6144]{0,1:T(8,128)(2,1)}) %all-reduce.5.cloned.1.call-update) | async-done | bytes 3145744 | tf_op jit(solution)/shard_map/psum | solution.py:82
  644.0 0.0 copy-done.5
  644.0 0.0 copy-done.7
  644.0 1.6 fusion.28
  645.5 43.4 %reduce-scatter.2.cloned.1.call-done = bf16[128,768]{1,0:T(8,128)(2,1)} async-done(((bf16[128,6144]{1,0:T(8,128)(2,1)}), bf16[128,768]{1,0:T(8,128)(2,1)}) %reduce-scatter.2.cloned.1.call-update) | async-done | bytes 196624 | tf_op jit(solution)/shard_map/reduce_scatter | solution.py:88
  (4 shorter events, 0.0 us)
Async XLA Ops:
  7.2 139.7 %copy-start = (bf16[1,256,128]{2,1,0:T(8,128)(2,1)S(1)}, bf16[1,256,128]{2,1,0:T(8,128)(2,1)}, u32[]{:S(2)}) copy-start(bf16[1,256,128]{2,1,0:T(8,128)(2,1)} %param.10) | copy-start | bytes 196612
  7.2 49.5 %all-gather.7.cloned.1.call-start = ((), (), s32[]{:S(2)}) async-start(), calls=%async_computation.2 | async-start | bytes 1769472 | tf_op jit(solution)/shard_map/all_gather | solution.py:51
  7.9 135.5 %all-gather.5.cloned.1.call-start = ((), (), s32[]{:S(2)}) async-start(), calls=%async_computation.1 | async-start | bytes 3244032 | tf_op jit(solution)/shard_map/all_gather | solution.py:70
  8.7 196.8 %all-gather.9.cloned.1.call-start = ((), (), s32[]{:S(2)}) async-start(), calls=%async_computation.3 | async-start | bytes 5308416 | tf_op jit(solution)/shard_map/all_gather | solution.py:50
  9.4 370.2 %all-reduce.3.cloned.1.call-start = ((), (), s32[]{:S(2)}) async-start(), calls=%async_computation.4 | async-start | bytes 6291456 | tf_op jit(solution)/shard_map/psum | solution.py:82
  11.5 135.6 %copy-start.8 = (bf16[1,256,128]{2,1,0:T(8,128)(2,1)S(1)}, bf16[1,256,128]{2,1,0:T(8,128)(2,1)}, u32[]{:S(2)}) copy-start(bf16[1,256,128]{2,1,0:T(8,128)(2,1)} %param.8) | copy-start | bytes 196612
  11.5 135.8 %copy-start.9 = (bf16[1,256,128]{2,1,0:T(8,128)(2,1)S(1)}, bf16[1,256,128]{2,1,0:T(8,128)(2,1)}, u32[]{:S(2)}) copy-start(bf16[1,256,128]{2,1,0:T(8,128)(2,1)} %param.9) | copy-start | bytes 196612
  211.4 168.2 %copy-start.4 = (bf16[256,192]{0,1:T(8,128)(2,1)S(1)}, bf16[256,192]{0,1:T(8,128)(2,1)}, u32[]{:S(2)}) copy-start(bf16[256,192]{0,1:T(8,128)(2,1)} %param.7) | copy-start | bytes 294916
  211.4 255.8 %copy-start.3 = (bf16[1,128,6144]{2,1,0:T(8,128)(2,1)S(1)}, bf16[1,128,6144]{2,1,0:T(8,128)(2,1)}, u32[]{:S(2)}) copy-start(bf16[1,128,6144]{2,1,0:T(8,128)(2,1)} %all-gather.7.cloned.1.call-done) | copy-start | bytes 4718596
  211.4 255.8 %all-gather.11.cloned.1.call-start = ((), (), s32[]{:S(2)}) async-start(), calls=%async_computation.5 | async-start | bytes 3244032 | tf_op jit(solution)/shard_map/all_gather | solution.py:70
  380.5 90.0 %copy-start.6 = (bf16[256,192]{0,1:T(8,128)(2,1)}, bf16[256,192]{0,1:T(8,128)(2,1)S(1)}, u32[]{:S(2)}) copy-start(bf16[256,192]{0,1:T(8,128)(2,1)S(1)} %add_convert_fusion.1) | copy-start | bytes 294916
  380.5 3.2 collective-permute-start
  384.4 259.6 %all-reduce.5.cloned.1.call-start = ((), (), s32[]{:S(2)}) async-start(), calls=%async_computation.6 | async-start | bytes 6291456 | tf_op jit(solution)/shard_map/psum | solution.py:82
  477.0 1.9 copy-start.1
  477.0 212.0 %reduce-scatter.2.cloned.1.call-start = ((), (), s32[]{:S(2)}) async-start(), calls=%async_computation.7 | async-start | bytes 1769472 | tf_op jit(solution)/shard_map/reduce_scatter | solution.py:88
  478.8 1.9 copy-start.2
  480.7 163.2 %copy-start.5 = (bf16[256,192]{0,1:T(8,128)(2,1)S(1)}, bf16[256,192]{0,1:T(8,128)(2,1)}, u32[]{:S(2)}) copy-start(bf16[256,192]{0,1:T(8,128)(2,1)} %broadcast_select_fusion) | copy-start | bytes 294916
  480.7 163.2 %copy-start.7 = (bf16[256,192]{0,1:T(8,128)(2,1)S(1)}, bf16[256,192]{0,1:T(8,128)(2,1)}, u32[]{:S(2)}) copy-start(bf16[256,192]{0,1:T(8,128)(2,1)} %copy-done.6) | copy-start | bytes 294916
Sparse Core Ops, SparseCore 0:
  10.1 46.5 all-gather.6
  60.4 82.9 all-gather.4
  145.5 59.8 all-gather.8
  211.5 167.9 all-reduce.2
  384.5 82.6 all-gather.10
  477.1 166.8 all-reduce.4
  647.4 41.5 reduce-scatter.1
where the time goes:
time: 696 us
  waiting for transfers between devices  648 us (93%)
  matrix products  24.6 us (4%)
  between operations  14.3 us (2%)
    psum x2, waiting for transfers between devices, per_device(): lax.psum(head_term.astype(jnp.bfloat16), 'tensor').astype(jnp.float32)  329 us
    all_gather x2, waiting for transfers between devices, per_device(): whole = lax.all_gather(incoming, 'tensor', axis=1, tiled=True)  169 us
    all_gather x1, waiting for transfers between devices, per_device(): lax.all_gather(w_qkv, 'dp', axis=1, tiled=True)  57.7 us
    all_gather x1, waiting for transfers between devices, per_device(): lax.all_gather(w_out, 'dp', axis=2, tiled=True)  45.2 us
    reduce_scatter x1, waiting for transfers between devices, per_device(): lax.psum_scatter(grad_acc.astype(jnp.bfloat16), 'dp', scatter_dimension=1...  43.4 us
    dot_general x13, matrix products, contract(): lax.dot_general(left, right, (((left_dim,), (right_dim,)), ((), ())), pre...  23.9 us
  transfers between devices with their start and end apart: 8, of which 8 were waited for; matrix products, arithmetic and copies ran while one was open for 2% of the time, Pallas kernels for 0%

commit v1 on v0

--- a/solution.py
+++ b/solution.py
@@ -47,7 +47,15 @@
     head_index = lax.axis_index("tensor")
     width = grad_out.shape[1]
     qkv_full, out_full = (
-        lax.all_gather(w_qkv, "dp", axis=1, tiled=True),
+        jnp.concatenate(
+            jax.lax.all_to_all(
+                jnp.stack([w_qkv for _ in range(jax.lax.axis_size("dp"))], axis=0),
+                concat_axis=0,
+                split_axis=0,
+                axis_name="dp",
+            ),
+            axis=1,
+        ),
         lax.all_gather(w_out, "dp", axis=2, tiled=True),
     )
     proj_in = qkv_full[0]

time: 696 us -> 672 us (0.966)
  waiting for transfers between devices: 648 us -> 614 us
  starting transfers between devices: 1.57 us -> 8.78 us
    all_gather x1 -> x0, waiting for transfers between devices: 57.7 us -> none  [per_device(): lax.all_gather(w_qkv, 'dp', axis=1, tiled=True)]
    all_gather x1, waiting for transfers between devices: 45.2 us -> 71.1 us  [per_device(): lax.all_gather(w_out, 'dp', axis=2, tiled=True)]
    all_to_all x0 -> x1, starting transfers between devices: none -> 7.24 us  [per_device(): jax.lax.all_to_all(jnp.stack([w_qkv for _ in range(jax.lax.axis_size('dp'...]
  transfers between devices with their start and end apart: 8 -> 8, of which waited for: 8 -> 7; matrix products, arithmetic and copies ran while one was open for 2% -> 2% of each run, Pallas kernels for 0% -> 0%
where the time goes in v1:
time: 672 us; the launch traced here: 671 us
  waiting for transfers between devices  614 us (91%)
  matrix products  23.4 us (3%)
  between operations  14.3 us (2%)
  starting transfers between devices  8.78 us (1%)
    psum x2, waiting for transfers between devices, per_device(): lax.psum(head_term.astype(jnp.bfloat16), 'tensor').astype(jnp.float32)  328 us
    all_gather x2, waiting for transfers between devices, per_device(): whole = lax.all_gather(incoming, 'tensor', axis=1, tiled=True)  170 us
    all_gather x1, waiting for transfers between devices, per_device(): lax.all_gather(w_out, 'dp', axis=2, tiled=True)  71.1 us
    reduce_scatter x1, waiting for transfers between devices, per_device(): lax.psum_scatter(grad_acc.astype(jnp.bfloat16), 'dp', scatter_dimension=1...  43.3 us
    dot_general x13, matrix products, contract(): lax.dot_general(left, right, (((left_dim,), (right_dim,)), ((), ())), pre...  22.7 us
  transfers between devices with their start and end apart: 8, of which 7 were waited for; matrix products, arithmetic and copies ran while one was open for 2% of the time, Pallas kernels for 0%

profile of v1, /device:TPU:6, one launch (start us, length us, event | category | flops | bytes accessed | tf_op | source)
XLA Modules:
  0.0 671.3 jit_solution(7230417291575023361)
XLA Ops:
  7.2 0.0 copy-start
  7.2 0.0 all-gather.6.cloned.1.call-start
  7.2 0.7 all-gather.6.cloned.1.call-update
  7.9 3.7 stack.2
  11.6 0.0 copy-start.4
  11.6 0.0 copy-start.10
  11.6 0.0 copy-start.8
  11.6 7.2 %all-to-all-start = ((bf16[8,1,768,384]{3,2,1,0:T(8,128)(2,1)}), bf16[8,1,768,384]{3,2,1,0:T(8,128)(2,1)}, u32[]{:S(2)}, u32[]{:S(2)}) async-start(bf16[8,1,768,384]{3,2,1,0:T(8,128)(2,1)} %stack.2), calls=%async_computation | async-start | bytes 9437184 | tf_op jit(solution)/shard_map/all_to_all | solution.py:51
  18.9 0.0 all-gather.4.cloned.1.call-start
  18.9 0.0 copy-done.4
  18.9 0.7 broadcast_select_fusion.1
  19.6 0.0 all-gather.4.cloned.1.call-update
  19.6 0.0 all-reduce.3.cloned.1.call-start
  19.7 0.0 copy-done.10
  19.7 0.2 reduce_window_sum.11
  19.9 0.1 fusion.38
  19.9 0.0 copy-done.8
  20.0 0.0 copy-done.9
  20.0 0.2 fusion.47
  20.2 0.1 fusion.14
  20.3 71.1 %all-gather.6.cloned.1.call-done = bf16[1,128,6144]{2,1,0:T(8,128)(2,1)} async-done(((bf16[1,128,768]{2,1,0:T(8,128)(2,1)}), bf16[1,128,6144]{2,1,0:T(8,128)(2,1)}) %all-gather.6.cloned.1.call-update) | async-done | bytes 1572880 | tf_op jit(solution)/shard_map/all_gather | solution.py:59
  91.3 87.0 %all-gather.4.cloned.1.call-done = bf16[256,6144]{0,1:T(8,128)(2,1)} async-done(((bf16[256,192]{0,1:T(8,128)(2,1)}), bf16[256,6144]{0,1:T(8,128)(2,1)}) %all-gather.4.cloned.1.call-update) | async-done | bytes 3145744 | tf_op jit(solution)/shard_map/all_gather | solution.py:78
  178.3 3.4 fusion.7
  181.7 0.0 copy-done
  181.7 0.2 multiply_reduce_fusion.1
  181.9 0.1 multiply_convert_fusion.1
  182.0 0.2 convolution_convert_fusion.7
  182.2 0.2 convolution_convert_fusion.8
  182.4 0.2 convolution_convert_fusion.6
  182.6 0.0 all-to-all-done
  182.6 5.8 convolution_convert_fusion.1
  188.4 0.0 all-reduce.3.cloned.1.call-update
  188.4 0.0 all-gather.8.cloned.1.call-start
  188.5 166.9 %all-reduce.3.cloned.1.call-done = bf16[256,6144]{0,1:T(8,128)(2,1)} async-done(((bf16[256,6144]{0,1:T(8,128)(2,1)}), bf16[256,6144]{0,1:T(8,128)(2,1)}) %all-reduce.3.cloned.1.call-update) | async-done | bytes 3145744 | tf_op jit(solution)/shard_map/psum | solution.py:90
  355.4 0.9 add_convert_fusion.1
  356.3 0.0 copy-start.6
  356.3 1.3 collective-permute-start
  357.6 1.9 collective-permute-done
  359.5 0.7 broadcast_select_fusion
  360.2 0.0 all-gather.8.cloned.1.call-update
  360.2 0.0 all-reduce.5.cloned.1.call-start
  360.2 82.7 %all-gather.8.cloned.1.call-done = bf16[256,6144]{0,1:T(8,128)(2,1)} async-done(((bf16[256,192]{0,1:T(8,128)(2,1)}), bf16[256,6144]{0,1:T(8,128)(2,1)}) %all-gather.8.cloned.1.call-update) | async-done | bytes 3145744 | tf_op jit(solution)/shard_map/all_gather | solution.py:78
  443.0 0.0 copy-done.3
  443.0 2.9 fusion.10
  445.9 0.2 convolution_convert_fusion.3
  446.1 0.2 multiply_reduce_fusion
  446.3 0.0 copy-done.6
  446.3 0.1 multiply_convert_fusion
  446.4 0.2 convolution_convert_fusion.4
  446.6 0.2 convolution_convert_fusion.5
  446.8 5.8 convolution_convert_fusion
  452.6 0.0 all-reduce.5.cloned.1.call-update
  452.6 0.0 reduce-scatter.2.cloned.1.call-start
  452.7 0.2 convolution_convert_fusion.2
  452.9 1.6 copy-done.1
  454.5 1.2 convolution_select_fusion.1
  455.7 0.7 copy-done.2
  456.4 2.3 fusion.1
  458.7 0.0 reduce-scatter.2.cloned.1.call-update
  458.7 160.9 %all-reduce.5.cloned.1.call-done = bf16[256,6144]{0,1:T(8,128)(2,1)} async-done(((bf16[256,6144]{0,1:T(8,128)(2,1)}), bf16[256,6144]{0,1:T(8,128)(2,1)}) %all-reduce.5.cloned.1.call-update) | async-done | bytes 3145744 | tf_op jit(solution)/shard_map/psum | solution.py:90
  619.6 0.0 copy-done.5
  619.6 0.0 copy-done.7
  619.6 1.6 fusion.26
  621.2 43.3 %reduce-scatter.2.cloned.1.call-done = bf16[128,768]{1,0:T(8,128)(2,1)} async-done(((bf16[128,6144]{1,0:T(8,128)(2,1)}), bf16[128,768]{1,0:T(8,128)(2,1)}) %reduce-scatter.2.cloned.1.call-update) | async-done | bytes 196624 | tf_op jit(solution)/shard_map/reduce_scatter | solution.py:96
  (6 shorter events, 0.0 us)
Async XLA Ops:
  7.2 174.5 %copy-start = (bf16[1,256,128]{2,1,0:T(8,128)(2,1)S(1)}, bf16[1,256,128]{2,1,0:T(8,128)(2,1)}, u32[]{:S(2)}) copy-start(bf16[1,256,128]{2,1,0:T(8,128)(2,1)} %param.10) | copy-start | bytes 196612
  7.2 84.1 %all-gather.6.cloned.1.call-start = ((), (), s32[]{:S(2)}) async-start(), calls=%async_computation.3 | async-start | bytes 1769472 | tf_op jit(solution)/shard_map/all_gather | solution.py:59
  11.6 7.3 %copy-start.4 = (bf16[256,192]{0,1:T(8,128)(2,1)S(1)}, bf16[256,192]{0,1:T(8,128)(2,1)}, u32[]{:S(2)}) copy-start(bf16[256,192]{0,1:T(8,128)(2,1)} %param.7) | copy-start | bytes 294916
  11.6 8.1 %copy-start.10 = (s32[1,3]{1,0:T(1,128)S(1)}, s32[1,3]{1,0:T(1,128)}, u32[]{:S(2)}) copy-start(s32[1,3]{1,0:T(1,128)} %param.13) | copy-start | bytes 40
  11.6 8.3 %copy-start.8 = (bf16[1,256,128]{2,1,0:T(8,128)(2,1)S(1)}, bf16[1,256,128]{2,1,0:T(8,128)(2,1)}, u32[]{:S(2)}) copy-start(bf16[1,256,128]{2,1,0:T(8,128)(2,1)} %param.8) | copy-start | bytes 196612
  11.6 8.3 %copy-start.9 = (bf16[1,256,128]{2,1,0:T(8,128)(2,1)S(1)}, bf16[1,256,128]{2,1,0:T(8,128)(2,1)}, u32[]{:S(2)}) copy-start(bf16[1,256,128]{2,1,0:T(8,128)(2,1)} %param.9) | copy-start | bytes 196612
  11.6 171.0 %all-to-all-start = ((bf16[8,1,768,384]{3,2,1,0:T(8,128)(2,1)}), bf16[8,1,768,384]{3,2,1,0:T(8,128)(2,1)}, u32[]{:S(2)}, u32[]{:S(2)}) async-start(bf16[8,1,768,384]{3,2,1,0:T(8,128)(2,1)} %stack.2), calls=%async_computation | async-start | bytes 9437184 | tf_op jit(solution)/shard_map/all_to_all | solution.py:51
  18.9 159.4 %all-gather.4.cloned.1.call-start = ((), (), s32[]{:S(2)}) async-start(), calls=%async_computation.2 | async-start | bytes 3244032 | tf_op jit(solution)/shard_map/all_gather | solution.py:78
  19.6 335.8 %all-reduce.3.cloned.1.call-start = ((), (), s32[]{:S(2)}) async-start(), calls=%async_computation.4 | async-start | bytes 6291456 | tf_op jit(solution)/shard_map/psum | solution.py:90
  188.4 254.6 %copy-start.3 = (bf16[1,128,6144]{2,1,0:T(8,128)(2,1)S(1)}, bf16[1,128,6144]{2,1,0:T(8,128)(2,1)}, u32[]{:S(2)}) copy-start(bf16[1,128,6144]{2,1,0:T(8,128)(2,1)} %all-gather.6.cloned.1.call-done) | copy-start | bytes 4718596
  188.4 254.6 %all-gather.8.cloned.1.call-start = ((), (), s32[]{:S(2)}) async-start(), calls=%async_computation.5 | async-start | bytes 3244032 | tf_op jit(solution)/shard_map/all_gather | solution.py:78
  356.3 90.0 %copy-start.6 = (bf16[256,192]{0,1:T(8,128)(2,1)}, bf16[256,192]{0,1:T(8,128)(2,1)S(1)}, u32[]{:S(2)}) copy-start(bf16[256,192]{0,1:T(8,128)(2,1)S(1)} %add_convert_fusion.1) | copy-start | bytes 294916
  356.3 3.2 collective-permute-start
  360.2 259.4 %all-reduce.5.cloned.1.call-start = ((), (), s32[]{:S(2)}) async-start(), calls=%async_computation.6 | async-start | bytes 6291456 | tf_op jit(solution)/shard_map/psum | solution.py:90
  452.6 1.9 copy-start.1
  452.6 211.8 %reduce-scatter.2.cloned.1.call-start = ((), (), s32[]{:S(2)}) async-start(), calls=%async_computation.7 | async-start | bytes 1769472 | tf_op jit(solution)/shard_map/reduce_scatter | solution.py:96
  454.5 1.9 copy-start.2
  456.4 163.2 %copy-start.5 = (bf16[256,192]{0,1:T(8,128)(2,1)S(1)}, bf16[256,192]{0,1:T(8,128)(2,1)}, u32[]{:S(2)}) copy-start(bf16[256,192]{0,1:T(8,128)(2,1)} %broadcast_select_fusion) | copy-start | bytes 294916
  456.4 163.2 %copy-start.7 = (bf16[256,192]{0,1:T(8,128)(2,1)S(1)}, bf16[256,192]{0,1:T(8,128)(2,1)}, u32[]{:S(2)}) copy-start(bf16[256,192]{0,1:T(8,128)(2,1)} %copy-done.6) | copy-start | bytes 294916
Sparse Core Ops, SparseCore 0:
  10.1 81.1 all-gather.5
  95.0 83.1 all-gather.3
  188.5 166.8 all-reduce.2
  360.3 82.6 all-gather.7
  452.7 166.8 all-reduce.4
  622.9 41.5 reduce-scatter.1
